TPU v7x, 512 devices: a whole 4x8x8 slice. The times are simulated.
512 devices in a mesh: grp: 16 (over y, x_hi), pos: 32 (over x_lo, z, core).
Axes of the slice: x: 4 (x_hi: 2, x_lo: 2; x = x_hi * 2 + x_lo), y: 8, z: 8, core: 2. Of those that a mesh axis runs over, the one named last changes fastest.
Arguments:
- features: bfloat16 [2, 2048, 512, 448], P(None, ('grp', 'pos'))
- channel_index: int32 [100], replicated, may hold values from 0 to 447, as said below
Outputs:
- factor: float32 [512, 100, 100], P('pos')
- mean_vec: float32 [512, 100], P('pos')
Inputs may be any that keep to these rules, and one draw needn't show every extreme that they name: `channel_index`: 100 distinct channel numbers; 0 and 447 are always among them.
All inputs are finite; a program needn't handle non-finite values.
Results may differ from a plain program's by a relative error of at most 0.0003.
Values may be sent and summed in bfloat16 or wider, within the bound.
A program may use at most 64 MiB of HBM per device.

v0:
```python
import jax
import jax.numpy as jnp
from jax import lax
from jax.sharding import PartitionSpec as P

RIDGE = 0.01


def moments(received):
    samples = received.reshape(received.shape[0], received.shape[2], received.shape[3])
    second_moment = jnp.einsum("ipc,ipd->pcd", samples, samples, preferred_element_type=jnp.float32)
    column_sums = jnp.sum(samples.astype(jnp.float32), axis=0)
    return (second_moment, column_sums)


def combine(second_moment, column_sums):
    return (
        lax.psum_scatter(second_moment, "grp", scatter_dimension=0, tiled=True),
        lax.psum_scatter(column_sums, "grp", scatter_dimension=0, tiled=True),
    )


def factorize(second_moment, column_sums, image_total):
    mean_vec = column_sums / image_total
    outer = image_total * mean_vec[:, :, None] * mean_vec[:, None, :]
    identity = jnp.eye(mean_vec.shape[1], dtype=jnp.float32)
    covariance = (second_moment - outer) / (image_total - 1) + RIDGE * identity
    return (jnp.linalg.cholesky(covariance), mean_vec)


def local(features, channel_index):
    pos_count = lax.axis_size("pos")
    grp_count = lax.axis_size("grp")
    batch_total, img_local, positions, width = features.shape
    keep_count = channel_index.shape[0]
    selector = (
        lax.broadcasted_iota(jnp.int32, (width, keep_count), 0) == channel_index[None, :]
    ).astype(jnp.bfloat16)
    image_total = batch_total * img_local * pos_count * grp_count
    chosen_list = []
    for batch_index in range(batch_total):
        flat = features[batch_index].reshape(img_local * positions, width)
        chosen = jnp.dot(flat, selector, preferred_element_type=jnp.float32).astype(jnp.bfloat16)
        chosen_list.append(chosen)
    partial_list = []
    for chosen in chosen_list:
        shaped = chosen.reshape(img_local, pos_count, positions // pos_count, keep_count)
        partial_list.append(
            moments(lax.all_to_all(shaped, "pos", split_axis=1, concat_axis=0, tiled=True))
        )
    shares = [combine(pair[0], pair[1]) for pair in partial_list]
    second_moment = shares[0][0]
    column_sums = shares[0][1]
    for pair in shares[1:]:
        second_moment = second_moment + pair[0]
        column_sums = column_sums + pair[1]
    factor, mean_vec = factorize(second_moment, column_sums, image_total)
    factor, mean_vec = (
        lax.all_gather(factor, "grp", axis=0, tiled=True),
        lax.all_gather(mean_vec, "grp", axis=0, tiled=True),
    )
    return (factor, mean_vec)


def solution(mesh):
    return jax.shard_map(
        local,
        mesh=mesh,
        in_specs=(P(None, ("grp", "pos"), None, None), P()),
        out_specs=(P("pos", None, None), P("pos", None)),
        check_vma=False,
    )
```

profile of v0, /device:TPU:64, one launch (start us, length us, event | category | flops | bytes accessed | tf_op | source)
XLA Modules:
  0.0 289.7 jit_solution(10344877939015737435)
XLA Ops:
  7.2 2.4 fusion.10
  9.6 1.4 copy.28
  11.0 0.0 copy-start
  11.0 0.5 copy.44
  11.5 0.1 copy-done
  11.7 0.5 fusion
  12.1 0.3 copy.29
  12.4 0.9 copy.30
  13.3 11.1 %all-to-all-start = ((bf16[4,32,16,100]{3,2,0,1:T(8,128)(2,1)}), bf16[4,32,16,100]{3,2,0,1:T(8,128)(2,1)S(1)}, u32[]{:S(2)}, u32[]{:S(2)}) async-start(bf16[4,32,16,100]{3,2,0,1:T(8,128)(2,1)} %copy.30), calls=%async_computation | async-start | bytes 1048576 | tf_op jit(solution)/shard_map/all_to_all | solution.py:49
  24.3 1.4 copy.33
  25.7 0.5 copy.45
  26.3 0.5 fusion.1
  26.7 0.3 copy.34
  27.0 0.9 copy.35
  27.9 14.2 %all-to-all-done = bf16[4,32,16,100]{3,2,0,1:T(8,128)(2,1)S(1)} async-done(((bf16[4,32,16,100]{3,2,0,1:T(8,128)(2,1)}), bf16[4,32,16,100]{3,2,0,1:T(8,128)(2,1)S(1)}, u32[]{:S(2)}, u32[]{:S(2)}) %all-to-all-start) | async-done | bytes 409632 | tf_op jit(solution)/shard_map/all_to_all | solution.py:49
  42.1 4.5 %all-to-all-start.1 = ((bf16[4,32,16,100]{3,2,0,1:T(8,128)(2,1)}), bf16[4,32,16,100]{3,2,0,1:T(8,128)(2,1)S(1)}, u32[]{:S(2)}, u32[]{:S(2)}) async-start(bf16[4,32,16,100]{3,2,0,1:T(8,128)(2,1)} %copy.35), calls=%async_computation.1 | async-start | bytes 1048576 | tf_op jit(solution)/shard_map/all_to_all | solution.py:49
  46.6 0.0 reduce-scatter.4.cloned.1.call-start
  46.6 0.4 fusion.3
  47.0 17.4 %all-to-all-done.1 = bf16[4,32,16,100]{3,2,0,1:T(8,128)(2,1)S(1)} async-done(((bf16[4,32,16,100]{3,2,0,1:T(8,128)(2,1)}), bf16[4,32,16,100]{3,2,0,1:T(8,128)(2,1)S(1)}, u32[]{:S(2)}, u32[]{:S(2)}) %all-to-all-start.1) | async-done | bytes 409632 | tf_op jit(solution)/shard_map/all_to_all | solution.py:49
  64.4 0.4 convolution_add_fusion
  64.9 1.2 copy.38
  66.1 0.0 reduce-scatter.4.cloned.1.call-update
  66.1 1.3 dynamic-slice
  67.4 0.2 convert_reduce_fusion
  67.6 0.2 convert_reduce_fusion.1
  67.7 42.8 %all-reduce.1 = f32[16,100]{1,0:T(8,128)S(1)} all-reduce(f32[16,100]{1,0:T(8,128)S(1)} %add.31), channel_id=5, replica_groups=mesh['grp'=16,'pos'=32] {'grp'}, use_global_device_ids=true, to_apply=%region_3.0.clone | all-reduce | flops 1600 | bytes 12800
  110.5 0.7 fusion.8
  111.2 35.3 %all-gather = f32[16,1,100]{2,1,0:T(1,128)S(1)} all-gather(f32[1,1,100]{2,1,0:T(1,128)S(1)} %get-tuple-element.10), channel_id=1, replica_groups=mesh['grp'=16,'pos'=32] {'grp'}, dimensions={0}, use_global_device_ids=true | all-gather | bytes 6800 | tf_op jit(solution)/shard_map/all_gather | solution.py:60
  146.5 0.7 broadcast_multiply_fusion
  147.2 78.3 %reduce-scatter.4.cloned.1.call-done = f32[1,100,100]{1,2,0:T(8,128)} async-done(((f32[16,100,100]{1,2,0:T(8,128)}), f32[1,100,100]{1,2,0:T(8,128)}) %reduce-scatter.4.cloned.1.call-update) | async-done | bytes 40016
  225.5 0.9 select_add_fusion
  226.4 0.1 copy.39
  226.5 0.9 fusion.7
  227.4 9.1 %custom-call.4 = f32[1,100,100]{2,1,0:T(8,128)S(1)} custom-call(f32[1,100,100]{2,1,0:T(8,128)S(1)} %fusion.7), custom_call_target="Cholesky" | custom-call | tf_op jit(solution)/shard_map/jit(cholesky)/cholesky | solution.py:28
  236.6 0.1 copy.40
  236.7 0.1 select_reduce_fusion
  236.8 0.6 compare_reduce_fusion
  237.4 0.7 select_select_fusion
  238.1 0.1 copy.42
  238.2 43.0 %all_gather.6 = f32[16,100,100]{2,1,0:T(8,128)S(1)} all-gather(f32[1,100,100]{2,1,0:T(8,128)S(1)} %copy.42), channel_id=1, replica_groups=mesh['grp'=16,'pos'=32] {'grp'}, dimensions={0}, use_global_device_ids=true | all-gather | bytes 680000 | tf_op jit(solution)/shard_map/all_gather | solution.py:59
  281.2 1.0 copy.43
  282.3 0.6 copy.51
  (1 shorter events, 0.0 us)
Async XLA Ops:
  11.0 0.7 copy-start
  13.3 28.8 %all-to-all-start = ((bf16[4,32,16,100]{3,2,0,1:T(8,128)(2,1)}), bf16[4,32,16,100]{3,2,0,1:T(8,128)(2,1)S(1)}, u32[]{:S(2)}, u32[]{:S(2)}) async-start(bf16[4,32,16,100]{3,2,0,1:T(8,128)(2,1)} %copy.30), calls=%async_computation | async-start | bytes 1048576 | tf_op jit(solution)/shard_map/all_to_all | solution.py:49
  42.1 22.3 %all-to-all-start.1 = ((bf16[4,32,16,100]{3,2,0,1:T(8,128)(2,1)}), bf16[4,32,16,100]{3,2,0,1:T(8,128)(2,1)S(1)}, u32[]{:S(2)}, u32[]{:S(2)}) async-start(bf16[4,32,16,100]{3,2,0,1:T(8,128)(2,1)} %copy.35), calls=%async_computation.1 | async-start | bytes 1048576 | tf_op jit(solution)/shard_map/all_to_all | solution.py:49
  46.6 178.9 %reduce-scatter.4.cloned.1.call-start = ((), (), s32[]{:S(2)}) async-start(), calls=%async_computation.3 | async-start | bytes 905216
Sparse Core Ops, SparseCore 0:
  66.3 159.2 reduce-scatter.3
where the time goes:
time: 290 us
  blocking collectives  121 us (42%)
  waiting for transfers between devices  110 us (38%)
  starting transfers between devices  15.6 us (5%)
  between operations  14.2 us (5%)
  other arithmetic  14 us (5%)
  local copies, waits for them, and re-layouts  13.2 us (5%)
    unnamed x2, waiting for transfers between devices  78.3 us
    all_gather x1, blocking collectives, local(): lax.all_gather(factor, 'grp', axis=0, tiled=True)  43 us
    unnamed x1, blocking collectives  42.8 us
    all_gather x1, blocking collectives, local(): lax.all_gather(mean_vec, 'grp', axis=0, tiled=True)  35.3 us
    all_to_all x2, waiting for transfers between devices, local(): lax.all_to_all(shaped, 'pos', split_axis=1, concat_axis=0, tiled=True)  31.6 us
    all_to_all x2, starting transfers between devices, local(): lax.all_to_all(shaped, 'pos', split_axis=1, concat_axis=0, tiled=True)  15.5 us
    another operation x3, other arithmetic, factorize(): return (jnp.linalg.cholesky(covariance), mean_vec)  9.91 us
  transfers between devices with their start and end apart: 3, of which 3 were waited for; matrix products, arithmetic and copies ran while one was open for 2% of the time, Pallas kernels for 0%

commit v1 on v0

--- a/solution.py
+++ b/solution.py
@@ -4,6 +4,13 @@
 from jax.sharding import PartitionSpec as P
 
 RIDGE = 0.01
+
+
+def exchange_blocks(x, axis, split, join):
+    count = lax.axis_size(axis)
+    blocks = jnp.stack(jnp.split(x, count, axis=split), axis=0)
+    blocks = lax.all_to_all(blocks, axis, split_axis=0, concat_axis=0)
+    return jnp.concatenate(blocks, axis=join)
 
 
 def moments(received):
@@ -45,9 +52,7 @@
     partial_list = []
     for chosen in chosen_list:
         shaped = chosen.reshape(img_local, pos_count, positions // pos_count, keep_count)
-        partial_list.append(
-            moments(lax.all_to_all(shaped, "pos", split_axis=1, concat_axis=0, tiled=True))
-        )
+        partial_list.append(moments(exchange_blocks(shaped, "pos", 1, 0)))
     shares = [combine(pair[0], pair[1]) for pair in partial_list]
     second_moment = shares[0][0]
     column_sums = shares[0][1]

time: 290 us -> 317 us (1.093)
  local copies, waits for them, and re-layouts: 13.2 us -> 50.1 us
  waiting for transfers between devices: 110 us -> 95.6 us
  starting transfers between devices: 15.6 us -> 19.4 us
    unnamed x7 -> x69, local copies, waits for them, and re-layouts: 4.08 us -> 41.5 us
    all_to_all x2, waiting for transfers between devices: 31.6 us -> 17.3 us  [exchange_blocks(): blocks = lax.all_to_all(blocks, axis, split_axis=0, concat_axis=0)]
    all_to_all x2, starting transfers between devices: 15.5 us -> 19.4 us  [exchange_blocks(): blocks = lax.all_to_all(blocks, axis, split_axis=0, concat_axis=0)]
  transfers between devices with their start and end apart: 3 -> 3, of which waited for: 3 -> 2; matrix products, arithmetic and copies ran while one was open for 2% -> 8% of each run, Pallas kernels for 0% -> 0%
where the time goes in v1:
time: 317 us; the launch traced here: 316 us
  blocking collectives  121 us (38%)
  waiting for transfers between devices  95.6 us (30%)
  local copies, waits for them, and re-layouts  50.1 us (16%)
  starting transfers between devices  19.4 us (6%)
  between operations  14.2 us (4%)
  other arithmetic  14 us (4%)
    unnamed x2, waiting for transfers between devices  78.3 us
    all_gather x1, blocking collectives, local(): lax.all_gather(factor, 'grp', axis=0, tiled=True)  43 us
    unnamed x1, blocking collectives  42.9 us
    unnamed x69, local copies, waits for them, and re-layouts  41.5 us
    all_gather x1, blocking collectives, local(): lax.all_gather(mean_vec, 'grp', axis=0, tiled=True)  35.3 us
    all_to_all x2, starting transfers between devices, exchange_blocks(): blocks = lax.all_to_all(blocks, axis, split_axis=0, concat_axis=0)  19.4 us
    all_to_all x2, waiting for transfers between devices, exchange_blocks(): blocks = lax.all_to_all(blocks, axis, split_axis=0, concat_axis=0)  17.3 us
    another operation x3, other arithmetic, factorize(): return (jnp.linalg.cholesky(covariance), mean_vec)  9.91 us
  transfers between devices with their start and end apart: 3, of which 2 were waited for; matrix products, arithmetic and copies ran while one was open for 8% of the time, Pallas kernels for 0%

profile of v1, /device:TPU:64, one launch (start us, length us, event | category | flops | bytes accessed | tf_op | source)
XLA Modules:
  0.0 316.4 jit_solution(1173992517850667759)
XLA Ops:
  7.2 2.4 fusion.10
  9.6 1.4 copy.148
  12.4 0.6 constant_dynamic-update-slice_fusion.31
  13.0 0.6 constant_dynamic-update-slice_fusion.30
  13.6 0.6 constant_dynamic-update-slice_fusion.29
  14.2 0.6 constant_dynamic-update-slice_fusion.28
  14.8 0.6 constant_dynamic-update-slice_fusion.27
  15.4 0.6 constant_dynamic-update-slice_fusion.26
  16.1 0.6 constant_dynamic-update-slice_fusion.25
  16.7 0.6 constant_dynamic-update-slice_fusion.24
  17.3 0.6 constant_dynamic-update-slice_fusion.23
  17.9 0.6 constant_dynamic-update-slice_fusion.22
  18.5 0.6 constant_dynamic-update-slice_fusion.21
  19.1 0.6 constant_dynamic-update-slice_fusion.20
  19.7 0.6 constant_dynamic-update-slice_fusion.19
  20.3 0.6 constant_dynamic-update-slice_fusion.18
  20.9 0.6 constant_dynamic-update-slice_fusion.17
  21.5 0.6 constant_dynamic-update-slice_fusion.16
  22.1 0.6 constant_dynamic-update-slice_fusion.15
  22.7 0.6 constant_dynamic-update-slice_fusion.14
  23.3 0.6 constant_dynamic-update-slice_fusion.13
  24.0 0.6 constant_dynamic-update-slice_fusion.12
  24.6 0.6 constant_dynamic-update-slice_fusion.11
  25.2 0.6 constant_dynamic-update-slice_fusion.10
  25.8 0.6 constant_dynamic-update-slice_fusion.9
  26.4 0.6 constant_dynamic-update-slice_fusion.8
  27.0 0.6 constant_dynamic-update-slice_fusion.7
  27.6 0.6 constant_dynamic-update-slice_fusion.6
  28.2 0.6 constant_dynamic-update-slice_fusion.5
  28.8 0.6 constant_dynamic-update-slice_fusion.4
  29.4 0.6 constant_dynamic-update-slice_fusion.3
  30.0 0.6 constant_dynamic-update-slice_fusion.2
  30.6 0.6 constant_dynamic-update-slice_fusion.1
  31.2 0.6 constant_dynamic-update-slice_fusion
  31.9 11.1 %all-to-all-start = ((bf16[32,4,1,16,100]{4,3,1,2,0:T(8,128)(2,1)}), bf16[32,4,1,16,100]{4,3,1,2,0:T(8,128)(2,1)S(1)}, u32[]{:S(2)}, u32[]{:S(2)}) async-start(bf16[32,4,1,16,100]{4,3,1,2,0:T(8,128)(2,1)} %constant_dynamic-update-slice_fusion), calls=%async_computation | async-start | bytes 1048576 | tf_op jit(solution)/shard_map/all_to_all | solution.py:12
  42.9 1.4 copy.182
  46.2 0.6 constant_dynamic-update-slice_fusion.62
  47.4 0.6 constant_dynamic-update-slice_fusion.60
  49.8 0.6 constant_dynamic-update-slice_fusion.56
  52.2 0.6 constant_dynamic-update-slice_fusion.52
  52.9 0.6 constant_dynamic-update-slice_fusion.51
  54.1 0.6 constant_dynamic-update-slice_fusion.49
  56.5 0.6 constant_dynamic-update-slice_fusion.45
  57.1 0.6 constant_dynamic-update-slice_fusion.44
  58.9 0.6 constant_dynamic-update-slice_fusion.41
  60.1 0.6 constant_dynamic-update-slice_fusion.39
  61.3 0.6 constant_dynamic-update-slice_fusion.37
  62.5 0.6 constant_dynamic-update-slice_fusion.35
  64.9 8.3 %all-to-all-start.1 = ((bf16[32,4,1,16,100]{4,3,1,2,0:T(8,128)(2,1)}), bf16[32,4,1,16,100]{4,3,1,2,0:T(8,128)(2,1)S(1)}, u32[]{:S(2)}, u32[]{:S(2)}) async-start(bf16[32,4,1,16,100]{4,3,1,2,0:T(8,128)(2,1)} %constant_dynamic-update-slice_fusion.32), calls=%async_computation.1 | async-start | bytes 1048576 | tf_op jit(solution)/shard_map/all_to_all | solution.py:12
  73.7 17.3 %all-to-all-done.1 = bf16[32,4,1,16,100]{4,3,1,2,0:T(8,128)(2,1)S(1)} async-done(((bf16[32,4,1,16,100]{4,3,1,2,0:T(8,128)(2,1)}), bf16[32,4,1,16,100]{4,3,1,2,0:T(8,128)(2,1)S(1)}, u32[]{:S(2)}, u32[]{:S(2)}) %all-to-all-start.1) | async-done | bytes 409632 | tf_op jit(solution)/shard_map/all_to_all | solution.py:12
  91.4 1.2 copy.216
  92.7 1.3 dynamic-slice
  94.3 42.9 %all-reduce.1 = f32[16,100]{1,0:T(8,128)S(1)} all-reduce(f32[16,100]{1,0:T(8,128)S(1)} %add.31), channel_id=5, replica_groups=mesh['grp'=16,'pos'=32] {'grp'}, use_global_device_ids=true, to_apply=%region_3.0.clone | all-reduce | flops 1600 | bytes 12800
  137.2 0.7 fusion.8
  137.8 35.3 %all-gather = f32[16,1,100]{2,1,0:T(1,128)S(1)} all-gather(f32[1,1,100]{2,1,0:T(1,128)S(1)} %get-tuple-element.10), channel_id=1, replica_groups=mesh['grp'=16,'pos'=32] {'grp'}, dimensions={0}, use_global_device_ids=true | all-gather | bytes 6800 | tf_op jit(solution)/shard_map/all_gather | solution.py:65
  173.2 0.7 broadcast_multiply_fusion
  173.8 78.3 %reduce-scatter.4.cloned.1.call-done = f32[1,100,100]{1,2,0:T(8,128)} async-done(((f32[16,100,100]{1,2,0:T(8,128)}), f32[1,100,100]{1,2,0:T(8,128)}) %reduce-scatter.4.cloned.1.call-update) | async-done | bytes 40016
  252.2 0.9 select_add_fusion
  253.2 0.9 fusion.7
  254.1 9.1 %custom-call.4 = f32[1,100,100]{2,1,0:T(8,128)S(1)} custom-call(f32[1,100,100]{2,1,0:T(8,128)S(1)} %fusion.7), custom_call_target="Cholesky" | custom-call | tf_op jit(solution)/shard_map/jit(cholesky)/cholesky | solution.py:35
  263.4 0.6 compare_reduce_fusion
  264.1 0.7 select_select_fusion
  264.9 43.0 %all_gather.6 = f32[16,100,100]{2,1,0:T(8,128)S(1)} all-gather(f32[1,100,100]{2,1,0:T(8,128)S(1)} %copy.220), channel_id=1, replica_groups=mesh['grp'=16,'pos'=32] {'grp'}, dimensions={0}, use_global_device_ids=true | all-gather | bytes 680000 | tf_op jit(solution)/shard_map/all_gather | solution.py:64
  307.9 1.0 copy.221
  (41 shorter events, 16.9 us)
Async XLA Ops:
  11.0 0.7 copy-start
  31.9 33.0 %all-to-all-start = ((bf16[32,4,1,16,100]{4,3,1,2,0:T(8,128)(2,1)}), bf16[32,4,1,16,100]{4,3,1,2,0:T(8,128)(2,1)S(1)}, u32[]{:S(2)}, u32[]{:S(2)}) async-start(bf16[32,4,1,16,100]{4,3,1,2,0:T(8,128)(2,1)} %constant_dynamic-update-slice_fusion), calls=%async_computation | async-start | bytes 1048576 | tf_op jit(solution)/shard_map/all_to_all | solution.py:12
  64.9 26.1 %all-to-all-start.1 = ((bf16[32,4,1,16,100]{4,3,1,2,0:T(8,128)(2,1)}), bf16[32,4,1,16,100]{4,3,1,2,0:T(8,128)(2,1)S(1)}, u32[]{:S(2)}, u32[]{:S(2)}) async-start(bf16[32,4,1,16,100]{4,3,1,2,0:T(8,128)(2,1)} %constant_dynamic-update-slice_fusion.32), calls=%async_computation.1 | async-start | bytes 1048576 | tf_op jit(solution)/shard_map/all_to_all | solution.py:12
  73.2 178.9 %reduce-scatter.4.cloned.1.call-start = ((), (), s32[]{:S(2)}) async-start(), calls=%async_computation.3 | async-start | bytes 905216
Sparse Core Ops, SparseCore 0:
  92.8 159.3 reduce-scatter.3
